TPU v7x, 256 devices: a whole 4x4x8 slice. The times are simulated.
256 devices in a mesh: row: 16 (over z_hi, y, core), col: 16 (over x, z_lo).
Axes of the slice: x: 4, y: 4, z: 8 (z_hi: 2, z_lo: 4; z = z_hi * 4 + z_lo), core: 2. Of those that a mesh axis runs over, the one named last changes fastest.
Arguments:
- cost_rough: bfloat16 [33792, 33792], P('row', 'col'), may hold values from 0.0009994507 to 1
- land_mask: int32 [176, 192], P('row', 'col'), may hold values 0 or 1
- wage_start: float32 [176, 192, 256], P('row', 'col'), may hold values from -3 to 3
- tech_start: float32 [176, 192, 256], P('row', 'col'), may hold values from -3 to 3
- temp_start: float32 [176, 192, 256], P('row', 'col'), may hold values from -2.5 to 2.5
- damping: float32 [1], replicated, may hold values from 0.3 to 0.8
Outputs:
- wage_field: float32 [176, 192, 256], P('row', 'col')
- tech_field: float32 [176, 192, 256], P('row', 'col')
- temp_field: float32 [176, 192, 256], P('row', 'col')
All inputs are finite; a program needn't handle non-finite values. No bound on the sum of `land_mask` on one device may be relied on, other than what follows from the above.
Results may differ from a plain program's by a relative error of at most 0.0003.
Values may be sent and summed in bfloat16 or wider, within the bound.
A program may use at most 128 MiB of HBM per device.

v0:
```python
import jax
import jax.numpy as jnp
from jax import lax
from jax.sharding import PartitionSpec as P

LAT = 176
LON = 192
ITERS = 3
ELL = 44


def padded_2(cells, sides, width):
    for axis, dim in sides:
        count = lax.axis_size(axis)
        ends = count - 1
        head = lax.slice_in_dim(cells, 0, width, axis=dim)
        tail = lax.slice_in_dim(cells, cells.shape[dim] - width, cells.shape[dim], axis=dim)
        cells = jnp.concatenate(
            [
                lax.ppermute(tail, axis, [(i, (i + 1) % count) for i in range(ends)]),
                cells,
                lax.ppermute(head, axis, [((i + 1) % count, i) for i in range(ends)]),
            ],
            axis=dim,
        )
    return cells


def cost_block(rough_block, destin, source):
    distance = (
        jnp.abs(destin[:, None] // LON - source[None, :] % LAT)
        + jnp.abs(destin[:, None] % LON - source[None, :] // LAT)
    ).astype(jnp.float32)
    scaled = rough_block.astype(jnp.float32) * jnp.exp(-distance / ELL) / (ELL * ELL)
    return scaled.astype(jnp.bfloat16)


def laplace(padded, field):
    return padded[2:, 1:-1] + padded[:-2, 1:-1] + padded[1:-1, 2:] + padded[1:-1, :-2] - 4.0 * field


def local(cost_rough, land_mask, wage_start, tech_start, temp_start, damping):
    height, breadth = cost_rough.shape
    band_lat, band_lon, scenarios = wage_start.shape
    source = lax.axis_index("col") * breadth + jnp.arange(breadth, dtype=jnp.int32)
    lat_first = lax.axis_index("row") * band_lat

    def build_row(pair):
        rough_row, lat_offset = pair
        destin = (lat_first + lat_offset) * LON + jnp.arange(LON, dtype=jnp.int32)
        return cost_block(rough_row, destin, source)

    slabs = lax.map(
        build_row,
        (cost_rough.reshape(band_lat, LON, breadth), jnp.arange(band_lat, dtype=jnp.int32)),
    )
    cost_tile = slabs.reshape(height, breadth)
    share = 0.25 + land_mask.astype(jnp.float32)[:, :, None]
    wage_field, tech_field, temp_field = (wage_start, tech_start, temp_start)
    for iteration in range(ITERS):
        supply = (jnp.exp(tech_field - wage_field) * share).astype(jnp.bfloat16)
        gathered = lax.all_gather(supply, "row", axis=0, tiled=True)
        columns = gathered.transpose(1, 0, 2).reshape(breadth, scenarios)
        product = jnp.dot(cost_tile, columns, preferred_element_type=jnp.float32).reshape(
            band_lat, LON, scenarios
        )
        access = lax.psum_scatter(product, "col", scatter_dimension=1, tiled=True)
        target = 0.5 * (jnp.log(access) + tech_field)
        wage_field = wage_field + damping[0] * (target - wage_field)
        stacked = jnp.stack((tech_field, temp_field))
        padded = padded_2(stacked, (("row", 1), ("col", 2)), 1)
        tech_next = (
            tech_field + 0.2 * laplace(padded[0], tech_field) - 0.05 * temp_field * temp_field
        )
        temp_next = (
            temp_field + 0.2 * laplace(padded[1], temp_field) + 0.5 * share * jnp.tanh(wage_field)
        )
        tech_field, temp_field = (tech_next, temp_next)
    return (wage_field, tech_field, temp_field)


def solution(mesh):
    in_specs = (
        P("row", "col"),
        P("row", "col"),
        P("row", "col", None),
        P("row", "col", None),
        P("row", "col", None),
        P(),
    )
    out_specs = (P("row", "col", None), P("row", "col", None), P("row", "col", None))
    return jax.shard_map(local, mesh=mesh, in_specs=in_specs, out_specs=out_specs, check_vma=False)
```

profile of v0, /device:TPU:1, one launch (start us, length us, event | category | flops | bytes accessed | tf_op | source)
XLA Modules:
  0.0 740.6 jit_solution(5490739183297818805)
XLA Ops:
  9.8 47.8 %while.15 = (s32[]{:T(128)}, bf16[11,192,2112]{2,1,0:T(8,128)(2,1)}, bf16[11,192,2112]{2,1,0:T(8,128)(2,1)}, s32[11]{0:T(128)S(1)}, s32[]{:T(128)}, /*index=5*/s32[]{:T(128)}, s32[]{:T(128)}, s32[]{:T(128)}) while((s32[]{:T(128)}, bf16[11,192,2112]{2,1,0:T(8,128)(2,1)}, bf16[11,192,2112]{2,1,0:T(8,128)(2,1)}, ...), condition=%wide.region_1.2_spmd.clone.clone, body=%wide.region_0.1_spmd.clone.clone.sunk | while | flops 4898116 | bytes 1712901 | solution.py:53
  11.0 3.1 fusion.66
  15.3 3.1 fusion.66
  19.7 3.1 fusion.66
  24.0 3.0 fusion.66
  28.3 3.1 fusion.66
  32.6 3.1 fusion.66
  37.0 3.1 fusion.66
  41.3 3.1 fusion.66
  45.6 3.1 fusion.66
  49.9 3.3 fusion.66
  54.5 3.1 fusion.66
  57.6 16.2 %all-gather.4.cloned.1.call-done = bf16[176,12,256]{2,1,0:T(8,128)(2,1)} async-done(((bf16[11,12,256]{2,1,0:T(8,128)(2,1)}), bf16[176,12,256]{2,1,0:T(8,128)(2,1)}) %all-gather.4.cloned.1.call-update) | async-done | bytes 1081360 | tf_op jit(solution)/shard_map/all_gather | solution.py:62
  75.5 7.8 %fusion.56 = f32[11,192,256]{2,1,0:T(8,128)} fusion(bf16[11,192,2112]{2,1,0:T(8,128)(2,1)} %get-tuple-element.124, bf16[2112,256,1]{1,0,2:T(8,128)(2,1)S(1)} %bitcast.73), kind=kOutput, calls=%fused_computation.113 | convolution fusion | flops 2283798528 | bytes 12165120 | tf_op jit(solution)/shard_map/dot_general | solution.py:64
  84.3 3.0 collective-permute-start
  89.2 3.3 collective-permute-done.1
  97.3 2.0 collective-permute-done.3
  99.4 147.4 %all-reduce.7.cloned.1.call-done = f32[11,192,256]{2,1,0:T(8,128)} async-done(((f32[11,192,256]{2,1,0:T(8,128)}), f32[11,192,256]{2,1,0:T(8,128)}) %all-reduce.7.cloned.1.call-update) | async-done | bytes 2162704
  248.8 67.7 %all-gather.6.cloned.1.call-done = bf16[176,12,256]{2,1,0:T(8,128)(2,1)} async-done(((bf16[11,12,256]{2,1,0:T(8,128)(2,1)}), bf16[176,12,256]{2,1,0:T(8,128)(2,1)}) %all-gather.6.cloned.1.call-update) | async-done | bytes 1081360 | tf_op jit(solution)/shard_map/all_gather | solution.py:62
  318.2 7.8 %fusion.57 = f32[11,192,256]{2,1,0:T(8,128)} fusion(bf16[11,192,2112]{2,1,0:T(8,128)(2,1)} %get-tuple-element.124, bf16[2112,256,1]{1,0,2:T(8,128)(2,1)S(1)} %bitcast.75), kind=kOutput, calls=%fused_computation.114 | convolution fusion | flops 2283798528 | bytes 12165120 | tf_op jit(solution)/shard_map/dot_general | solution.py:64
  326.1 3.0 collective-permute-start.4
  331.0 3.3 collective-permute-done.5
  337.2 4.9 collective-permute-done.7
  342.3 146.3 %all-reduce.9.cloned.1.call-done = f32[11,192,256]{2,1,0:T(8,128)} async-done(((f32[11,192,256]{2,1,0:T(8,128)}), f32[11,192,256]{2,1,0:T(8,128)}) %all-reduce.9.cloned.1.call-update) | async-done | bytes 2162704
  490.6 68.4 %all-gather.8.cloned.1.call-done = bf16[176,12,256]{2,1,0:T(8,128)(2,1)} async-done(((bf16[11,12,256]{2,1,0:T(8,128)(2,1)}), bf16[176,12,256]{2,1,0:T(8,128)(2,1)}) %all-gather.8.cloned.1.call-update) | async-done | bytes 1081360 | tf_op jit(solution)/shard_map/all_gather | solution.py:62
  560.7 7.7 %fusion.58 = f32[11,192,256]{2,1,0:T(8,128)} fusion(bf16[11,192,2112]{2,1,0:T(8,128)(2,1)} %get-tuple-element.124, bf16[2112,256,1]{1,0,2:T(8,128)(2,1)S(1)} %bitcast.74), kind=kOutput, calls=%fused_computation.115 | convolution fusion | flops 2283798528 | bytes 12165120 | tf_op jit(solution)/shard_map/dot_general | solution.py:64
  568.4 3.0 collective-permute-start.8
  571.4 1.9 collective-permute-start.9
  573.4 3.3 collective-permute-done.9
  579.6 4.9 collective-permute-done.11
  584.6 147.2 %all-reduce.11.cloned.1.call-done = f32[11,192,256]{2,1,0:T(8,128)} async-done(((f32[11,192,256]{2,1,0:T(8,128)}), f32[11,192,256]{2,1,0:T(8,128)}) %all-reduce.11.cloned.1.call-update) | async-done | bytes 2162704
  731.7 2.0 fusion.18
  (102 shorter events, 33.6 us)
Async XLA Ops:
  7.2 66.6 %all-gather.4.cloned.1.call-start = ((), (), s32[]{:S(2)}) async-start(), calls=%async_computation | async-start | bytes 1531904 | tf_op jit(solution)/shard_map/all_gather | solution.py:62
  9.7 237.1 %all-reduce.7.cloned.1.call-start = ((), (), s32[]{:S(2)}) async-start(), calls=%async_computation.3 | async-start | bytes 4325376
  83.3 0.9 copy-start
  83.3 1.0 copy-start.1
  83.3 12.8 %copy-start.3 = (u32[256]{0:T(256)S(1)}, u32[256]{0:T(256)}, u32[]{:S(2)}) copy-start(u32[256]{0:T(256)} %constant.114) | copy-start | bytes 3076
  83.3 163.5 %copy-start.2 = (f32[11,12,256]{2,1,0:T(8,128)S(1)}, f32[11,12,256]{2,1,0:T(8,128)}, u32[]{:S(2)}) copy-start(f32[11,12,256]{2,1,0:T(8,128)} %param.10) | copy-start | bytes 405508
  83.3 233.2 %all-gather.6.cloned.1.call-start = ((), (), s32[]{:S(2)}) async-start(), calls=%async_computation.1 | async-start | bytes 1531904 | tf_op jit(solution)/shard_map/all_gather | solution.py:62
  84.3 4.9 collective-permute-start
  87.3 5.2 collective-permute-start.1
  92.5 4.7 collective-permute-start.2
  94.1 5.2 collective-permute-start.3
  248.7 239.8 %all-reduce.9.cloned.1.call-start = ((), (), s32[]{:S(2)}) async-start(), calls=%async_computation.4 | async-start | bytes 4325376
  326.0 233.0 %all-gather.8.cloned.1.call-start = ((), (), s32[]{:S(2)}) async-start(), calls=%async_computation.2 | async-start | bytes 1531904 | tf_op jit(solution)/shard_map/all_gather | solution.py:62
  326.1 4.9 collective-permute-start.4
  329.1 5.2 collective-permute-start.5
  334.4 2.8 collective-permute-start.6
  335.9 6.2 collective-permute-start.7
  490.4 241.3 %all-reduce.11.cloned.1.call-start = ((), (), s32[]{:S(2)}) async-start(), calls=%async_computation.5 | async-start | bytes 4325376
  568.4 4.9 collective-permute-start.8
  571.4 5.2 collective-permute-start.9
  576.7 2.8 collective-permute-start.10
  578.3 6.2 collective-permute-start.11
Sparse Core Ops, SparseCore 0:
  11.3 62.4 all-gather.3
  83.4 163.3 all-reduce.6
  250.1 66.3 all-gather.5
  326.1 162.3 all-reduce.8
  491.7 67.3 all-gather.7
  568.5 163.1 all-reduce.10
where the time goes:
time: 750 us; the launch traced here: 741 us
  waiting for transfers between devices  615 us (82%)
  other arithmetic  43.6 us (6%)
  starting transfers between devices  23.6 us (3%)
  matrix products  23.2 us (3%)
  between operations  15.7 us (2%)
  local copies, waits for them, and re-layouts  13.1 us (2%)
    unnamed x9, waiting for transfers between devices  441 us
    all_gather x3, waiting for transfers between devices, local(): gathered = lax.all_gather(supply, 'row', axis=0, tiled=True)  152 us
    dynamic_update_slice x11, other arithmetic, local(): lax.map(build_row, (cost_rough.reshape(band_lat, LON, breadth), jnp.arang...  34 us
    dot_general x3, matrix products, local(): jnp.dot(cost_tile, columns, preferred_element_type=jnp.float32)  23.2 us
    ppermute x6, waiting for transfers between devices, padded_2(): lax.ppermute(head, axis, [((i + 1) % count, i) for i in range(ends)])  21.7 us
  transfers between devices with their start and end apart: 18, of which 12 were waited for; matrix products, arithmetic and copies ran while one was open for 6% of the time, Pallas kernels for 0%

commit v1 on v0

v1 whole, which is shorter than its diff:
```python
import jax
import jax.numpy as jnp
from jax import lax
from jax.experimental import pallas as pl
from jax.experimental.pallas import tpu as pltpu
from jax.sharding import PartitionSpec as P

LAT = 176
LON = 192
ITERS = 3
ELL = 44
A = 11
B = 12
S = 256
H = 128
BLOCK = 528
K = 2112
GROUP = 704
PIECE = 48
FLAT = 144
MESH = pl.DeviceIdType.MESH
f32 = jnp.float32
STEPS = 1024.0
MIDDLE = 8192.0
LN2 = 0.6931471805599453


def encode(value):
    code = jnp.log(jnp.maximum(value, 1e-30)) * (STEPS / LN2) + MIDDLE
    return jnp.round(jnp.clip(code, -32767.0, 32767.0)).astype(jnp.int32).astype(jnp.int16)


def decode(code):
    return jnp.exp((code.astype(jnp.int32).astype(f32) - MIDDLE) * (LN2 / STEPS))


def kernel(
    rough, share, wage0, tech0, temp0, damping,
    wage, tech, temp,
    stage, cost, near, pick, gathered, columns, piece, product, codes, landed, flat, zcodes, zlanded,
    access, padded, halo_out, halo_in, tech_new,
    stage_sem, ag_send, ag_recv, x_send, x_recv, z_send, z_recv, halo_send, halo_recv,
):
    row, col = lax.axis_index("row"), lax.axis_index("col")
    zh, y, core = row // 8, (row // 2) % 4, row % 2
    x, zl = col // 4, col % 4

    def at_row(zh_, y_, core_):
        return zh_ * 8 + (y_ % 4) * 2 + core_

    def at_col(x_, zl_):
        return (x_ % 4) * 4 + zl_ % 4

    partner = (at_row(zh, y, 1 - core), col)
    across = (at_row(1 - zh, y, core), col)
    y_up, y_down = (at_row(zh, y + 1, core), col), (at_row(zh, y + 3, core), col)
    x_up, x_down = (row, at_col(x + 1, zl)), (row, at_col(x + 3, zl))
    z_peers = [(row, at_col(x, zl + d)) for d in (1, 2, 3)]
    halo_peers = [((row + 1) % 16, col), ((row + 15) % 16, col), (row, (col + 1) % 16), (row, (col + 15) % 16)]
    peers = [partner, across, y_up, y_down, x_up, x_down] + z_peers + halo_peers

    def load_rough(a):
        return pltpu.make_async_copy(rough.at[pl.ds(a * LON, LON), :], stage.at[a], stage_sem.at[a])

    for a in range(A):
        load_rough(a).start()
    barrier = pltpu.get_barrier_semaphore()
    for peer in peers:
        pl.semaphore_signal(barrier, inc=1, device_id=peer, device_id_type=MESH)
    wage[...] = wage0[...]
    tech[...] = tech0[...]
    temp[...] = temp0[...]
    piece[...] = jnp.zeros_like(piece)
    flat[...] = jnp.zeros_like(flat)
    pl.semaphore_wait(barrier, len(peers))

    def slot(it, zh_, y_, core_):
        start = pl.multiple_of(at_row(zh_, y_, core_) * PIECE, 16)
        return gathered.at[it, :, :, pl.ds(start, PIECE), :]

    def half(it, h, zh_, y_, core_):
        start = pl.multiple_of(at_row(zh_, y_, core_) * PIECE, 16)
        return gathered.at[it, h, :, pl.ds(start, PIECE), :]

    def ag(it, k, ref, peer):
        return pltpu.make_async_remote_copy(
            src_ref=ref, dst_ref=ref, send_sem=ag_send.at[it, k], recv_sem=ag_recv.at[it, k],
            device_id=peer, device_id_type=MESH,
        )

    def own_copies(it):
        mine = slot(it, zh, y, core)
        return [ag(it, k, mine, peer) for k, peer in enumerate((partner, across, y_up, y_down))]

    def halo_copies(it):
        return [
            pltpu.make_async_remote_copy(
                src_ref=halo_out.at[it, d], dst_ref=halo_in.at[it, d],
                send_sem=halo_send.at[it, d], recv_sem=halo_recv.at[it, d],
                device_id=peer, device_id_type=MESH,
            )
            for d, peer in enumerate(halo_peers)
        ]

    def send_supply(it):
        for a in range(A):
            value = jnp.exp(tech[a] - wage[a]) * jnp.concatenate([share[a]] * 2, axis=1)
            for h in range(2):
                for g in range(3):
                    piece[h, g, 4 * a : 4 * a + 4, :] = value[4 * g : 4 * g + 4, h * H : h * H + H]
        start = pl.multiple_of(row * PIECE, 16)
        gathered[it, :, :, pl.ds(start, PIECE), :] = piece[...].astype(jnp.bfloat16)
        for copy in own_copies(it):
            copy.start()

    def send_halo(it):
        for f, field in enumerate((tech, temp)):
            halo_out[it, 0, f, 0:B, :] = field[A - 1]
            halo_out[it, 1, f, 0:B, :] = field[0]
            for a in range(A):
                halo_out[it, 2, f, a : a + 1, :] = field[a, B - 1 : B, :]
                halo_out[it, 3, f, a : a + 1, :] = field[a, 0:1, :]
        for copy in halo_copies(it):
            copy.start()

    halo_out[...] = jnp.zeros_like(halo_out)
    send_supply(0)
    send_halo(0)

    spot = lax.broadcasted_iota(jnp.int32, (1, 16 * PIECE), 1)
    device = jnp.zeros_like(spot)
    for r in range(1, 16):
        device = device + (spot >= PIECE * r).astype(jnp.int32)
    rest = spot - PIECE * device
    target = (rest & 3) * LAT + A * device + (rest >> 2)
    target = jnp.where(rest < 4 * A, target, -1)

    def pick_rows(i, _):
        start = pl.multiple_of(i * 16, 16)
        rows = i * 16 + lax.broadcasted_iota(jnp.int32, (16, 16 * PIECE), 0)
        pick[pl.ds(start, 16), :] = jnp.where(rows == target, 1.0, 0.0).astype(jnp.bfloat16)
        return 0

    lax.fori_loop(0, GROUP // 16, pick_rows, 0)

    column = lax.broadcasted_iota(jnp.int32, (1, K), 1)
    local_b = jnp.zeros_like(column)
    for b in range(1, B):
        local_b = local_b + (column >= LAT * b).astype(jnp.int32)
    source_a = column - LAT * local_b
    source_b = col * B + local_b

    def near_rows(i, _):
        start = pl.multiple_of(i * 16, 16)
        rows = i * 16 + lax.broadcasted_iota(jnp.int32, (16, K), 0)
        near[pl.ds(start, 16), :] = jnp.exp(jnp.abs(rows - source_b).astype(f32) * (-1.0 / ELL))
        return 0

    lax.fori_loop(0, LON // 16, near_rows, 0)

    def cost_latitude(a, _):
        load_rough(a).wait()
        lat = jnp.exp(jnp.abs(row * A + a - source_a).astype(f32) * (-1.0 / ELL)) * (1.0 / (ELL * ELL))

        def cost_rows(i, _):
            start = pl.multiple_of(i * 16, 16)
            put = pl.multiple_of(a * 48 + (i % 3) * 16, 16)
            value = stage[a, pl.ds(start, 16), :].astype(f32) * (lat * near[pl.ds(start, 16), :])
            cost[i // 3, pl.ds(put, 16), :] = value.astype(jnp.bfloat16)
            return 0

        return lax.fori_loop(0, LON // 16, cost_rows, 0)

    lax.fori_loop(0, A, cost_latitude, 0)

    def x_copy(it, k):
        return pltpu.make_async_remote_copy(
            src_ref=codes.at[k], dst_ref=landed.at[it, k],
            send_sem=x_send.at[it, k], recv_sem=x_recv.at[it, k],
            device_id=x_up if k % 2 == 0 else x_down, device_id_type=MESH,
        )

    def z_copy(it, d):
        return pltpu.make_async_remote_copy(
            src_ref=zcodes.at[(zl + d) % 4], dst_ref=zlanded.at[it, d - 1],
            send_sem=z_send.at[it, d - 1], recv_sem=z_recv.at[it, d - 1],
            device_id=z_peers[d - 1], device_id_type=MESH,
        )

    def iteration(it, _):
        pending = own_copies(it)

        def forward(k, ref, peer):
            copy = ag(it, k, ref, peer)
            copy.start()
            pending.append(copy)

        def arrived(k, ref, peer):
            ag(it, k, ref, peer).wait_recv()

        other = 1 - zh
        below, above, far = slot(it, zh, y + 3, core), slot(it, zh, y + 1, core), slot(it, zh, y + 2, core)
        arrived(2, below, y_down)
        forward(4, half(it, 0, zh, y + 3, core), y_up)
        forward(5, below, partner)
        arrived(3, above, y_up)
        forward(6, half(it, 1, zh, y + 1, core), y_down)
        forward(7, above, partner)
        theirs = slot(it, other, y, core)
        arrived(1, theirs, across)
        forward(8, theirs, y_up)
        forward(9, theirs, y_down)
        forward(10, theirs, partner)
        arrived(4, half(it, 0, zh, y + 2, core), y_down)
        arrived(6, half(it, 1, zh, y + 2, core), y_up)
        forward(11, far, partner)
        below, above, far = slot(it, other, y + 3, core), slot(it, other, y + 1, core), slot(it, other, y + 2, core)
        arrived(8, below, y_down)
        forward(12, half(it, 0, other, y + 3, core), y_up)
        forward(13, below, partner)
        arrived(9, above, y_up)
        forward(14, half(it, 1, other, y + 1, core), y_down)
        forward(15, above, partner)
        arrived(12, half(it, 0, other, y + 2, core), y_down)
        arrived(14, half(it, 1, other, y + 2, core), y_up)
        forward(16, far, partner)
        for k, zh_, dy in (
            (0, zh, 0), (5, zh, 3), (7, zh, 1), (10, other, 0), (11, zh, 2), (13, other, 3), (15, other, 1), (16, other, 2)
        ):
            arrived(k, slot(it, zh_, y + dy, 1 - core), partner)

        def select(g, _):
            start = pl.multiple_of(g * GROUP, 16)
            block = jnp.concatenate([gathered[it, 0, g], gathered[it, 1, g]], axis=1)
            columns[pl.ds(start, GROUP), :] = jnp.dot(pick[...], block, preferred_element_type=f32).astype(jnp.bfloat16)
            return 0

        lax.fori_loop(0, 3, select, 0)

        def multiply(n, x_):
            product[n] = jnp.dot(cost[x_ % 4], columns[...], preferred_element_type=f32)

        def rows_of(i):
            return pl.ds(pl.multiple_of(i * 48, 16), 48)

        def code_half(k, n, h):
            def some(i, _):
                codes[k, rows_of(i), :] = encode(product[n, rows_of(i), h * H : h * H + H])
                return 0

            lax.fori_loop(0, A, some, 0)
            x_copy(it, k).start()

        def code_sum(k, n, h, j):
            def some(i, _):
                value = product[n, rows_of(i), h * H : h * H + H] + decode(landed[it, j, rows_of(i), :])
                codes[k, rows_of(i), :] = encode(value)
                return 0

            lax.fori_loop(0, A, some, 0)
            x_copy(it, k).start()

        multiply(2, x + 2)
        code_half(0, 2, 0)
        code_half(1, 2, 1)
        multiply(1, x + 1)
        code_half(2, 1, 1)
        multiply(3, x + 3)
        code_half(3, 3, 0)
        x_copy(it, 0).wait_recv()
        code_sum(4, 1, 0, 0)
        x_copy(it, 1).wait_recv()
        code_sum(5, 3, 1, 1)
        multiply(0, x)

        for copy in halo_copies(it):
            copy.wait_recv()
        for f, field in enumerate((tech, temp)):
            low = jnp.where(row == 0, 0.0, halo_in[it, 0, f, 0:B, :])
            high = jnp.where(row == 15, 0.0, halo_in[it, 1, f, 0:B, :])
            for a in range(A):
                padded[f, a, 1 : 1 + B, :] = field[a]
                padded[f, a, 0:1, :] = jnp.where(col == 0, 0.0, halo_in[it, 2, f, a : a + 1, :])
                padded[f, a, B + 1 : B + 2, :] = jnp.where(col == 15, 0.0, halo_in[it, 3, f, a : a + 1, :])
            for a in range(A):
                centre = field[a]
                below_ = low if a == 0 else padded[f, a - 1, 1 : 1 + B, :]
                above_ = high if a == A - 1 else padded[f, a + 1, 1 : 1 + B, :]
                lap = above_ + below_ + padded[f, a, 2 : 2 + B, :] + padded[f, a, 0:B, :] - 4.0 * centre
                tech_new[f, a] = centre + 0.2 * lap
        for a in range(A):
            tech_new[0, a] = tech_new[0, a] - 0.05 * temp[a] * temp[a]

        for k in (2, 3, 4, 5):
            x_copy(it, k).wait_recv()
        for a in range(A):
            rows = slice(48 * a, 48 * a + 48)
            for h, j, k in ((0, 3, 4), (1, 2, 5)):
                value = product[0, rows, h * H : h * H + H] + decode(landed[it, j, rows, :]) + decode(landed[it, k, rows, :])
                for z in range(4):
                    flat[z, B * a : B * a + B, h * H : h * H + H] = value[B * z : B * z + B, :]
        for z in range(4):
            zcodes[z] = encode(flat[z])
        for d in (2, 1, 3):
            z_copy(it, d).start()
        for d in (1, 3, 2):
            z_copy(it, d).wait_recv()
        total = flat[zl]
        for d in (1, 2, 3):
            total = total + decode(zlanded[it, d - 1])
        access[...] = total

        for a in range(A):
            target_ = 0.5 * (jnp.log(access[B * a : B * a + B, :]) + tech[a])
            wage_a = wage[a] + damping[0] * (target_ - wage[a])
            wage[a] = wage_a
            both = jnp.concatenate([share[a]] * 2, axis=1)
            temp[a] = tech_new[1, a] + 0.5 * both * jnp.tanh(wage_a)
            tech[a] = tech_new[0, a]

        @pl.when(it < ITERS - 1)
        def _():
            send_supply(it + 1)
            send_halo(it + 1)

        for copy in pending:
            copy.wait_send()
        for k in range(6):
            x_copy(it, k).wait_send()
        for d in (1, 2, 3):
            z_copy(it, d).wait_send()
        for copy in halo_copies(it):
            copy.wait_send()
        return 0

    lax.fori_loop(0, ITERS, iteration, 0)


def local(cost_rough, land_mask, wage_start, tech_start, temp_start, damping):
    share = jnp.broadcast_to(0.25 + land_mask.astype(f32)[:, :, None], (A, B, H))
    field = jax.ShapeDtypeStruct((A, B, S), f32)
    vmem = pl.BlockSpec(memory_space=pltpu.VMEM)
    dma = pltpu.SemaphoreType.DMA
    return pl.pallas_call(
        kernel,
        out_shape=(field, field, field),
        in_specs=[pl.BlockSpec(memory_space=pl.ANY), vmem, vmem, vmem, vmem, pl.BlockSpec(memory_space=pltpu.SMEM)],
        out_specs=(vmem, vmem, vmem),
        scratch_shapes=[
            pltpu.VMEM((A, LON, K), jnp.bfloat16),
            pltpu.VMEM((4, BLOCK, K), jnp.bfloat16),
            pltpu.VMEM((LON, K), f32),
            pltpu.VMEM((GROUP, 16 * PIECE), jnp.bfloat16),
            pltpu.VMEM((ITERS, 2, 3, 16 * PIECE, H), jnp.bfloat16),
            pltpu.VMEM((K, S), jnp.bfloat16),
            pltpu.VMEM((2, 3, PIECE, H), f32),
            pltpu.VMEM((4, BLOCK, S), f32),
            pltpu.VMEM((6, BLOCK, H), jnp.int16),
            pltpu.VMEM((ITERS, 6, BLOCK, H), jnp.int16),
            pltpu.VMEM((4, FLAT, S), f32),
            pltpu.VMEM((4, FLAT, S), jnp.int16),
            pltpu.VMEM((ITERS, 3, FLAT, S), jnp.int16),
            pltpu.VMEM((FLAT, S), f32),
            pltpu.VMEM((2, A, 16, S), f32),
            pltpu.VMEM((ITERS, 4, 2, 16, S), f32),
            pltpu.VMEM((ITERS, 4, 2, 16, S), f32),
            pltpu.VMEM((2, A, B, S), f32),
            dma((A,)),
            dma((ITERS, 17)), dma((ITERS, 17)),
            dma((ITERS, 6)), dma((ITERS, 6)),
            dma((ITERS, 3)), dma((ITERS, 3)),
            dma((ITERS, 4)), dma((ITERS, 4)),
        ],
        compiler_params=pltpu.CompilerParams(collective_id=0, has_side_effects=True, vmem_limit_bytes=60 * 1024 * 1024),
    )(cost_rough, share, wage_start, tech_start, temp_start, damping)


def solution(mesh):
    in_specs = (
        P("row", "col"),
        P("row", "col"),
        P("row", "col", None),
        P("row", "col", None),
        P("row", "col", None),
        P(),
    )
    out_specs = (P("row", "col", None), P("row", "col", None), P("row", "col", None))
    return jax.shard_map(local, mesh=mesh, in_specs=in_specs, out_specs=out_specs, check_vma=False)
```

time: 750 us -> 134 us (0.18); the launches traced: 741 us -> 134 us
  waiting for transfers between devices: 615 us -> 0 us
  Pallas kernels: 0 us -> 126 us
  other arithmetic: 43.6 us -> 0.7 us
  starting transfers between devices: 23.6 us -> 0 us
  matrix products: 23.2 us -> 0 us
  between operations: 15.7 us -> 1.29 us
  local copies, waits for them, and re-layouts: 13.1 us -> 5.54 us
    unnamed x9 -> x0, waiting for transfers between devices: 441 us -> none
    all_gather x3 -> x0, waiting for transfers between devices: 152 us -> none  [local(): gathered = lax.all_gather(supply, 'row', axis=0, tiled=True)]
    pallas_call x0 -> x1, Pallas kernels: none -> 126 us  [local(): pl.pallas_call(kernel, out_shape=(field, field, field), in_specs=[pl.Bloc...]
    dynamic_update_slice x11 -> x0, other arithmetic: 34 us -> none  [local(): lax.map(build_row, (cost_rough.reshape(band_lat, LON, breadth), jnp.arang...]
    dot_general x3 -> x0, matrix products: 23.2 us -> none  [local(): jnp.dot(cost_tile, columns, preferred_element_type=jnp.float32)]
    ppermute x12 -> x0, starting transfers between devices: 23.2 us -> none  [the longest x6 13.6 us: padded_2(): lax.ppermute(tail, axis, [(i, (i + 1) % count) for i in range(ends)])]
    ppermute x12 -> x0, waiting for transfers between devices: 21.7 us -> none  [the longest x6 21.7 us: padded_2(): lax.ppermute(head, axis, [((i + 1) % count, i) for i in range(ends)])]
  transfers between devices with their start and end apart: 18 -> 0, of which waited for: 12 -> 0; matrix products, arithmetic and copies ran while one was open for 6% -> 0% of each run, Pallas kernels for 0% -> 0%
where the time goes in v1:
time: 134 us
  Pallas kernels  126 us (94%)
  local copies, waits for them, and re-layouts  5.54 us (4%)
    pallas_call x1, Pallas kernels, local(): pl.pallas_call(kernel, out_shape=(field, field, field), in_specs=[pl.Bloc...  126 us
    unnamed x3, local copies, waits for them, and re-layouts  4.81 us

profile of v1, /device:TPU:1, one launch (start us, length us, event | category | flops | bytes accessed | tf_op | source)
XLA Modules:
  0.0 133.8 jit_solution(6582528922838529953)
XLA Ops:
  1.3 0.7 convert_add_fusion
  2.0 0.7 broadcast_in_dim.2.share
  2.7 126.3 %shard_map.85 = (f32[11,12,256]{2,1,0:T(8,128)}, f32[11,12,256]{2,1,0:T(8,128)}, f32[11,12,256]{2,1,0:T(8,128)}) custom-call(bf16[2112,2112]{1,0:T(8,128)(2,1)} %rough.1, f32[11,12,128]{2,1,0:T(8,128)} %broadcast_in_dim.2.share, f32[11,12,256]{2,1,0:T(8,128)} %wage0.1, f32[11,12,256]{2,1,0:T(8,128)} %tech0.1, f32[11,12,256]{2,1,0:T(8,128)} %temp0.1, ...), custom_call_target="tpu_custom_call" | custom-call | tf_op jit(solution)/shard_map/pallas_call | solution.py:344
  129.0 1.6 %copy.13 = f32[11,12,256]{2,1,0:T(8,128)} copy(f32[11,12,256]{2,1,0:T(8,128)} %get-tuple-element.6) | data formatting | bytes 270336
  130.6 1.6 %copy.14 = f32[11,12,256]{2,1,0:T(8,128)} copy(f32[11,12,256]{2,1,0:T(8,128)} %get-tuple-element.7) | data formatting | bytes 270336
  132.2 1.6 %copy.15 = f32[11,12,256]{2,1,0:T(8,128)} copy(f32[11,12,256]{2,1,0:T(8,128)} %get-tuple-element.8) | data formatting | bytes 270336

commit v2 on v1

v2 whole, which is shorter than its diff:
```python
import functools

import jax
import jax.numpy as jnp
from jax import lax
from jax.experimental import pallas as pl
from jax.experimental.pallas import tpu as pltpu
from jax.sharding import PartitionSpec as P

LAT = 176
LON = 192
ITERS = 3
ELL = 44
A = 11
B = 12
S = 256
H = 128
BLOCK = 528
K = 2112
PIECE = 48
SIDE = 8 * PIECE
WIDE = 3 * SIDE
WINDOWS = ((0, 768, 0), (640, 768, 64), (1408, 704, 0))
PARTS = ((0, 6), (6, 11))
FLAT = 144
MESH = pl.DeviceIdType.MESH
f32 = jnp.float32
STEPS = 1024.0
MIDDLE = 8192.0
LN2 = 0.6931471805599453


def encode(value):
    code = jnp.log(jnp.maximum(value, 1e-30)) * (STEPS / LN2) + MIDDLE
    return jnp.round(jnp.clip(code, -32767.0, 32767.0)).astype(jnp.int32).astype(jnp.int16)


def decode(code):
    return jnp.exp((code.astype(jnp.int32).astype(f32) - MIDDLE) * (LN2 / STEPS))


def kernel(
    rough, mask, wage0, tech0, temp0, damping,
    wage, tech, temp,
    stage, cost, near, pick, folded, share, gathered, piece, product, codes, landed, flat, zcodes, zlanded,
    padded, halo_out, halo_in, tech_new,
    start_sem, stage_sem, ag_send, ag_recv, x_send, x_recv, z_send, z_recv, halo_send, halo_recv,
):
    row, col = lax.axis_index("row"), lax.axis_index("col")
    zh, y, core = row // 8, (row // 2) % 4, row % 2
    x, zl = col // 4, col % 4

    def at_row(zh_, y_, core_):
        return zh_ * 8 + (y_ % 4) * 2 + core_

    def at_col(x_, zl_):
        return (x_ % 4) * 4 + zl_ % 4

    partner = (at_row(zh, y, 1 - core), col)
    across = (at_row(1 - zh, y, core), col)
    y_up, y_down = (at_row(zh, y + 1, core), col), (at_row(zh, y + 3, core), col)
    x_up, x_down = (row, at_col(x + 1, zl)), (row, at_col(x + 3, zl))
    z_peers = [(row, at_col(x, zl + d)) for d in (1, 2, 3)]
    halo_peers = [((row + 1) % 16, col), ((row + 15) % 16, col), (row, (col + 1) % 16), (row, (col + 15) % 16)]
    y_far = (at_row(zh, y + 2, core), col)
    peers = [partner, across, y_up, y_down, y_far, x_up, x_down] + z_peers + halo_peers

    def load_rough(a):
        return pltpu.make_async_copy(rough.at[pl.ds(a * LON, LON), :], stage.at[a], stage_sem.at[a])

    for a in range(A):
        load_rough(a).start()
    barrier = pltpu.get_barrier_semaphore()
    for peer in peers:
        pl.semaphore_signal(barrier, inc=1, device_id=peer, device_id_type=MESH)
    starts = [
        pltpu.make_async_copy(source, field, start_sem.at[n])
        for n, (source, field) in enumerate(((wage0, wage), (tech0, tech), (temp0, temp)))
    ]
    for copy in starts:
        copy.start()
    piece[...] = jnp.zeros_like(piece)
    flat[...] = jnp.zeros_like(flat)
    halo_out[...] = jnp.zeros_like(halo_out)
    diagonal = lax.broadcasted_iota(jnp.int32, (B, B), 0) == lax.broadcasted_iota(jnp.int32, (B, B), 1)
    for a in range(A):
        line = jnp.broadcast_to(mask[a : a + 1, :].astype(f32), (B, B))
        stand = jnp.sum(jnp.where(diagonal, line, 0.0), axis=1, keepdims=True)
        share[a] = jnp.broadcast_to(0.25 + stand, (B, S))

    spot = lax.broadcasted_iota(jnp.int32, (1, 16 * PIECE), 1)
    device = jnp.zeros_like(spot)
    for r in range(1, 16):
        device = device + (spot >= PIECE * r).astype(jnp.int32)
    rest = spot - PIECE * device
    target = (rest & 3) * LAT + A * device + (rest >> 2)
    target = jnp.where(rest < 4 * A, target, -4096)

    def pick_rows(i, _):
        start = pl.multiple_of(i * 16, 16)
        rows = i * 16 + lax.broadcasted_iota(jnp.int32, (16, 16 * PIECE), 0)
        for n, shift in enumerate((0, 64)):
            pick[n, pl.ds(start, 16), :] = jnp.where(rows == target + shift, 1.0, 0.0).astype(jnp.bfloat16)
        return 0

    lax.fori_loop(0, PIECE, pick_rows, 0)

    column = lax.broadcasted_iota(jnp.int32, (1, K), 1)
    local_b = jnp.zeros_like(column)
    for b in range(1, B):
        local_b = local_b + (column >= LAT * b).astype(jnp.int32)
    source_a = column - LAT * local_b
    source_b = col * B + local_b

    def near_rows(i, _):
        start = pl.multiple_of(i * 16, 16)
        rows = i * 16 + lax.broadcasted_iota(jnp.int32, (16, K), 0)
        near[pl.ds(start, 16), :] = jnp.exp(jnp.abs(rows - source_b).astype(f32) * (-1.0 / ELL))
        return 0

    lax.fori_loop(0, LON // 16, near_rows, 0)

    def cost_latitude(a, _):
        load_rough(a).wait()
        lat = jnp.exp(jnp.abs(row * A + a - source_a).astype(f32) * (-1.0 / ELL)) * (1.0 / (ELL * ELL))

        def cost_rows(i, _):
            start = pl.multiple_of(i * 16, 16)
            put = pl.multiple_of(a * 48 + (i % 3) * 16, 16)
            value = stage[a, pl.ds(start, 16), :].astype(f32) * (lat * near[pl.ds(start, 16), :])
            cost[i // 3, pl.ds(put, 16), :] = value.astype(jnp.bfloat16)
            return 0

        return lax.fori_loop(0, LON // 16, cost_rows, 0)

    lax.fori_loop(0, A, cost_latitude, 0)

    def fold(n):
        for g, (first, count, shift) in enumerate(WINDOWS):
            block = jnp.dot(
                cost[n, :, first : first + count], pick[1 if shift else 0, 0:count, :], preferred_element_type=f32
            ).astype(jnp.bfloat16)
            folded[n, 0, :, g * SIDE : g * SIDE + SIDE] = block[:, 0:SIDE]
            folded[n, 1, :, g * SIDE : g * SIDE + SIDE] = block[:, SIDE : 2 * SIDE]

    def slot(it, h, zh_, y_, core_):
        start = pl.multiple_of(((y_ % 4) * 2 + core_) * PIECE, 16)
        return gathered.at[it, zh_, h, :, pl.ds(start, PIECE), :]

    def ag(it, h, k, ref, peer):
        return pltpu.make_async_remote_copy(
            src_ref=ref, dst_ref=ref, send_sem=ag_send.at[it, h, k], recv_sem=ag_recv.at[it, h, k],
            device_id=peer, device_id_type=MESH,
        )

    other = 1 - zh

    def gather_copies(it, h):
        own, theirs = slot(it, h, zh, y, core), slot(it, h, other, y, core)
        table = [
            (0, own, across), (1, own, y_up), (2, own, y_down), (3, own, y_far), (4, own, partner),
            (5, theirs, y_up), (6, theirs, y_down), (7, theirs, y_far), (8, theirs, partner),
            (9, slot(it, h, zh, y + 3, core), partner), (10, slot(it, h, zh, y + 1, core), partner),
            (11, slot(it, h, zh, y + 2, core), partner),
            (12, slot(it, h, other, y + 3, core), partner), (13, slot(it, h, other, y + 1, core), partner),
            (14, slot(it, h, other, y + 2, core), partner),
        ]
        return [functools.partial(ag, it, h, *entry) for entry in table]

    def halo_copies(it):
        return [
            pltpu.make_async_remote_copy(
                src_ref=halo_out.at[it, d], dst_ref=halo_in.at[it, d],
                send_sem=halo_send.at[it, d], recv_sem=halo_recv.at[it, d],
                device_id=peer, device_id_type=MESH,
            )
            for d, peer in enumerate(halo_peers)
        ]

    def send_supply(it, h):
        for a in range(A):
            lanes = slice(h * H, h * H + H)
            value = jnp.exp(tech[a, :, lanes] - wage[a, :, lanes]) * share[a, :, lanes]
            for g in range(3):
                piece[h, g, 4 * a : 4 * a + 4, :] = value[4 * g : 4 * g + 4, :]
        start = pl.multiple_of((y * 2 + core) * PIECE, 16)
        gathered[it, zh, h, :, pl.ds(start, PIECE), :] = piece[h].astype(jnp.bfloat16)
        for copy in gather_copies(it, h)[0:5]:
            copy().start()

    def send_halo(it):
        for f, field in enumerate((tech, temp)):
            halo_out[it, 0, f, 0:B, :] = field[A - 1]
            halo_out[it, 1, f, 0:B, :] = field[0]
            for a in range(A):
                halo_out[it, 2, f, a : a + 1, :] = field[a, B - 1 : B, :]
                halo_out[it, 3, f, a : a + 1, :] = field[a, 0:1, :]
        for copy in halo_copies(it):
            copy.start()

    def supply_of(it, side):
        return jnp.concatenate([gathered[it, side, h].reshape(WIDE, H) for h in (0, 1)], axis=1)

    def gather(it, meanwhile):
        copies = [gather_copies(it, h) for h in (0, 1)]

        def arrived(h, k, zh_, dy, core_, peer):
            ag(it, h, k, slot(it, h, zh_, y + dy, core_), peer).wait_recv()

        def forward(h, *ks):
            for k in ks:
                copies[h][k]().start()

        def beside(h, side, first, then):
            arrived(h, first, side, 3, core, y_down)
            forward(h, then)
            arrived(h, first + 1, side, 1, core, y_up)
            forward(h, then + 1)

        def near_half(n, _):
            product[n] = jnp.dot(folded[(x + n) % 4, zh], supply_of(it, zh), preferred_element_type=f32)
            return 0

        def halves(first, last):
            lax.fori_loop(first, last, near_half, 0)

        for h in (0, 1):
            meanwhile(h, halves)
            beside(h, zh, 1, 9)
            arrived(h, 0, other, 0, core, across)
            forward(h, 5, 6, 7, 8)
            arrived(h, 3, zh, 2, core, y_far)
            forward(h, 11)
        meanwhile(2, halves)
        beside(0, other, 5, 12)
        for h in (0, 1):
            for k, dy in ((4, 0), (9, 3), (10, 1), (11, 2)):
                arrived(h, k, zh, dy, 1 - core, partner)
        meanwhile(3, halves)
        arrived(0, 7, other, 2, core, y_far)
        forward(0, 14)
        beside(1, other, 5, 12)
        meanwhile(4, halves)
        arrived(1, 7, other, 2, core, y_far)
        forward(1, 14)
        for h in (0, 1):
            for k, dy in ((8, 0), (12, 3), (13, 1), (14, 2)):
                arrived(h, k, other, dy, 1 - core, partner)

    def part_rows(p):
        return 48 * PARTS[p][0], 48 * (PARTS[p][1] - PARTS[p][0])

    def x_copy(it, h, k):
        size = part_rows((0, 1, 1, 0, 0, 1)[k])[1]
        return pltpu.make_async_remote_copy(
            src_ref=codes.at[h, k, 0:size, :], dst_ref=landed.at[it, h, k, 0:size, :],
            send_sem=x_send.at[it, h, k], recv_sem=x_recv.at[it, h, k],
            device_id=x_up if k % 2 == 0 else x_down, device_id_type=MESH,
        )

    def z_copy(it, h, d):
        return pltpu.make_async_remote_copy(
            src_ref=zcodes.at[h, (zl + d) % 4], dst_ref=zlanded.at[it, h, d - 1],
            send_sem=z_send.at[it, h, d - 1], recv_sem=z_recv.at[it, h, d - 1],
            device_id=z_peers[d - 1], device_id_type=MESH,
        )

    def multiply_near(n, halves):
        if n >= 3:
            halves(2 * n - 6, 2 * n - 4)

    def iteration(it, _):
        def multiply(n):
            product[n] = product[n] + jnp.dot(
                folded[(x + n) % 4, other], supply_of(it, other), preferred_element_type=f32
            )

        def code(h, k, n, landing=None):
            p = (0, 1, 1, 0, 0, 1)[k]
            first, size = part_rows(p)
            if landing is not None:
                x_copy(it, h, landing).wait_recv()

            def some(i, _):
                start = pl.multiple_of(i * 48, 16)
                value = product[n, pl.ds(first + start, 48), h * H : h * H + H]
                if landing is not None:
                    value = value + decode(landed[it, h, landing, pl.ds(start, 48), :])
                codes[h, k, pl.ds(start, 48), :] = encode(value)
                return 0

            lax.fori_loop(0, size // 48, some, 0)
            x_copy(it, h, k).start()

        def finish(h):
            for k in (2, 3, 4, 5):
                x_copy(it, h, k).wait_recv()
            for p, pair in enumerate(((3, 4), (2, 5))):
                for a in range(*PARTS[p]):
                    rows = slice(48 * (a - PARTS[p][0]), 48 * (a - PARTS[p][0]) + 48)
                    value = product[0, 48 * a : 48 * a + 48, h * H : h * H + H]
                    for k in pair:
                        value = value + decode(landed[it, h, k, rows, :])
                    for z in range(4):
                        flat[h, z, B * a : B * a + B, :] = value[B * z : B * z + B, :]
            for z in range(4):
                zcodes[h, z] = encode(flat[h, z])
            for d in (2, 1, 3):
                z_copy(it, h, d).start()

        multiply(2)
        code(0, 0, 2)
        code(0, 1, 2)
        send_halo(it)
        multiply(1)
        code(0, 2, 1)
        multiply(3)
        code(0, 3, 3)
        code(1, 0, 2)
        code(1, 1, 2)
        multiply(0)
        code(0, 4, 1, 0)
        code(0, 5, 3, 1)
        code(1, 2, 1)
        code(1, 3, 3)
        code(1, 4, 1, 0)
        code(1, 5, 3, 1)
        finish(0)
        finish(1)
        for copy in halo_copies(it):
            copy.wait_recv()
        for f, field in enumerate((tech, temp)):
            low = jnp.where(row == 0, 0.0, halo_in[it, 0, f, 0:B, :])
            high = jnp.where(row == 15, 0.0, halo_in[it, 1, f, 0:B, :])
            for a in range(A):
                padded[f, a, 1 : 1 + B, :] = field[a]
                padded[f, a, 0:1, :] = jnp.where(col == 0, 0.0, halo_in[it, 2, f, a : a + 1, :])
                padded[f, a, B + 1 : B + 2, :] = jnp.where(col == 15, 0.0, halo_in[it, 3, f, a : a + 1, :])
            for a in range(A):
                centre = field[a]
                below_ = low if a == 0 else padded[f, a - 1, 1 : 1 + B, :]
                above_ = high if a == A - 1 else padded[f, a + 1, 1 : 1 + B, :]
                lap = above_ + below_ + padded[f, a, 2 : 2 + B, :] + padded[f, a, 0:B, :] - 4.0 * centre
                tech_new[f, a] = centre + 0.2 * lap
        for a in range(A):
            tech_new[0, a] = tech_new[0, a] - 0.05 * temp[a] * temp[a]

        for h in (0, 1):
            for d in (1, 3, 2):
                z_copy(it, h, d).wait_recv()
            lanes = slice(h * H, h * H + H)
            total = flat[h, zl]
            for d in (1, 2, 3):
                total = total + decode(zlanded[it, h, d - 1])
            for a in range(A):
                target_ = 0.5 * (jnp.log(total[B * a : B * a + B, :]) + tech[a, :, lanes])
                wage_a = wage[a, :, lanes] + damping[0] * (target_ - wage[a, :, lanes])
                wage[a, :, lanes] = wage_a
                temp[a, :, lanes] = tech_new[1, a, :, lanes] + 0.5 * share[a, :, lanes] * jnp.tanh(wage_a)
                tech[a, :, lanes] = tech_new[0, a, :, lanes]

            @pl.when(it < ITERS - 1)
            def _():
                send_supply(it + 1, h)

        for copy in halo_copies(it):
            copy.wait_send()
        for h in (0, 1):
            for copy in gather_copies(it, h):
                copy().wait_send()
            for k in range(6):
                x_copy(it, h, k).wait_send()
            for d in (1, 2, 3):
                z_copy(it, h, d).wait_send()

        @pl.when(it < ITERS - 1)
        def _():
            gather(it + 1, multiply_near)

        return 0

    def build(n, halves):
        if n < 4:
            fold(n)
        else:
            halves(0, 4)

    pl.semaphore_wait(barrier, len(peers))
    for copy in starts:
        copy.wait()
    send_supply(0, 0)
    send_supply(0, 1)
    gather(0, build)
    lax.fori_loop(0, ITERS, iteration, 0)


def hand_on(*refs):
    for source, result in zip(refs[:3], refs[3:]):
        result[...] = source[...]


def local(cost_rough, land_mask, wage_start, tech_start, temp_start, damping):
    field = jax.ShapeDtypeStruct((A, B, S), f32)
    vmem = pl.BlockSpec(memory_space=pltpu.VMEM)
    hbm = pl.BlockSpec(memory_space=pl.ANY)
    dma = pltpu.SemaphoreType.DMA
    fields = pl.pallas_call(
        kernel,
        out_shape=(field, field, field),
        in_specs=[hbm, vmem, hbm, hbm, hbm, pl.BlockSpec(memory_space=pltpu.SMEM)],
        out_specs=(vmem, vmem, vmem),
        scratch_shapes=[
            pltpu.VMEM((A, LON, K), jnp.bfloat16),
            pltpu.VMEM((4, BLOCK, K), jnp.bfloat16),
            pltpu.VMEM((LON, K), f32),
            pltpu.VMEM((2, 16 * PIECE, 16 * PIECE), jnp.bfloat16),
            pltpu.VMEM((4, 2, BLOCK, WIDE), jnp.bfloat16),
            pltpu.VMEM((A, B, S), f32),
            pltpu.VMEM((ITERS, 2, 2, 3, SIDE, H), jnp.bfloat16),
            pltpu.VMEM((2, 3, PIECE, H), f32),
            pltpu.VMEM((4, BLOCK, S), f32),
            pltpu.VMEM((2, 6, 288, H), jnp.int16),
            pltpu.VMEM((ITERS, 2, 6, 288, H), jnp.int16),
            pltpu.VMEM((2, 4, FLAT, H), f32),
            pltpu.VMEM((2, 4, FLAT, H), jnp.int16),
            pltpu.VMEM((ITERS, 2, 3, FLAT, H), jnp.int16),
            pltpu.VMEM((2, A, 16, S), f32),
            pltpu.VMEM((ITERS, 4, 2, 16, S), f32),
            pltpu.VMEM((ITERS, 4, 2, 16, S), f32),
            pltpu.VMEM((2, A, B, S), f32),
            dma((3,)),
            dma((A,)),
            dma((ITERS, 2, 15)), dma((ITERS, 2, 15)),
            dma((ITERS, 2, 6)), dma((ITERS, 2, 6)),
            dma((ITERS, 2, 3)), dma((ITERS, 2, 3)),
            dma((ITERS, 4)), dma((ITERS, 4)),
        ],
        compiler_params=pltpu.CompilerParams(collective_id=0, has_side_effects=True, vmem_limit_bytes=60 * 1024 * 1024),
    )(cost_rough, land_mask, wage_start, tech_start, temp_start, damping)
    return pl.pallas_call(hand_on, out_shape=(field, field, field), in_specs=[vmem] * 3, out_specs=(vmem,) * 3)(*fields)


def solution(mesh):
    in_specs = (
        P("row", "col"),
        P("row", "col"),
        P("row", "col", None),
        P("row", "col", None),
        P("row", "col", None),
        P(),
    )
    out_specs = (P("row", "col", None), P("row", "col", None), P("row", "col", None))
    return jax.shard_map(local, mesh=mesh, in_specs=in_specs, out_specs=out_specs, check_vma=False)
```

time: 134 us -> 113 us (0.84)
  Pallas kernels: 126 us -> 112 us
  local copies, waits for them, and re-layouts: 5.54 us -> 0 us
    pallas_call x1 -> x2, Pallas kernels: 126 us -> 112 us  [the longest x1 110 us: local(): pl.pallas_call(kernel, out_shape=(field, field, field), in_specs=[hbm, vm...]
    unnamed x3 -> x0, local copies, waits for them, and re-layouts: 4.81 us -> none
where the time goes in v2:
time: 113 us
  Pallas kernels  112 us (99%)
  between operations  1.29 us (1%)
    pallas_call x1, Pallas kernels, local(): pl.pallas_call(kernel, out_shape=(field, field, field), in_specs=[hbm, vm...  110 us

profile of v2, /device:TPU:1, one launch (start us, length us, event | category | flops | bytes accessed | tf_op | source)
XLA Modules:
  0.0 112.9 jit_solution(4877158187372987016)
XLA Ops:
  1.3 109.7 %shard_map.85 = (f32[11,12,256]{2,1,0:T(8,128)}, f32[11,12,256]{2,1,0:T(8,128)}, f32[11,12,256]{2,1,0:T(8,128)}) custom-call(bf16[2112,2112]{1,0:T(8,128)(2,1)} %rough.1, s32[11,12]{1,0:T(8,128)} %mask.1, f32[11,12,256]{2,1,0:T(8,128)} %wage0.1, f32[11,12,256]{2,1,0:T(8,128)} %tech0.1, f32[11,12,256]{2,1,0:T(8,128)} %temp0.1, f32[1]{0:T(128)S(6)} %copy.9.damping), custom_call_target="tpu_custom_call" | custom-call | tf_op jit(solution)/shard_map/pallas_call | solution.py:407
  111.0 1.9 %shard_map.86 = (f32[11,12,256]{2,1,0:T(8,128)}, f32[11,12,256]{2,1,0:T(8,128)}, f32[11,12,256]{2,1,0:T(8,128)}) custom-call(f32[11,12,256]{2,1,0:T(8,128)} %get-tuple-element.6.refs_0_, f32[11,12,256]{2,1,0:T(8,128)} %get-tuple-element.7.refs_1_, f32[11,12,256]{2,1,0:T(8,128)} %get-tuple-element.8.refs_2_), custom_call_target="tpu_custom_call" | custom-call | tf_op jit(solution)/shard_map/pallas_call | solution.py:440

commit v3 on v2

--- a/solution.py
+++ b/solution.py
@@ -41,8 +41,8 @@
 
 def kernel(
     rough, mask, wage0, tech0, temp0, damping,
-    wage, tech, temp,
-    stage, cost, near, pick, folded, share, gathered, piece, product, codes, landed, flat, zcodes, zlanded,
+    wage_out, tech_out, temp_out,
+    wage, tech, temp, stage, cost, near, pick, folded, share, gathered, piece, product, codes, landed, flat, zcodes, zlanded,
     padded, halo_out, halo_in, tech_new,
     start_sem, stage_sem, ag_send, ag_recv, x_send, x_recv, z_send, z_recv, halo_send, halo_recv,
 ):
@@ -149,7 +149,7 @@
 
     def ag(it, h, k, ref, peer):
         return pltpu.make_async_remote_copy(
-            src_ref=ref, dst_ref=ref, send_sem=ag_send.at[it, h, k], recv_sem=ag_recv.at[it, h, k],
+            src_ref=ref, dst_ref=ref, send_sem=ag_send.at[h, k], recv_sem=ag_recv.at[it % 2, h, k],
             device_id=peer, device_id_type=MESH,
         )
 
@@ -171,7 +171,7 @@
         return [
             pltpu.make_async_remote_copy(
                 src_ref=halo_out.at[it, d], dst_ref=halo_in.at[it, d],
-                send_sem=halo_send.at[it, d], recv_sem=halo_recv.at[it, d],
+                send_sem=halo_send.at[d], recv_sem=halo_recv.at[it % 2, d],
                 device_id=peer, device_id_type=MESH,
             )
             for d, peer in enumerate(halo_peers)
@@ -233,16 +233,16 @@
             forward(h, 11)
         meanwhile(2, halves)
         beside(0, other, 5, 12)
+        arrived(0, 7, other, 2, core, y_far)
+        forward(0, 14)
         for h in (0, 1):
             for k, dy in ((4, 0), (9, 3), (10, 1), (11, 2)):
                 arrived(h, k, zh, dy, 1 - core, partner)
         meanwhile(3, halves)
-        arrived(0, 7, other, 2, core, y_far)
-        forward(0, 14)
         beside(1, other, 5, 12)
-        meanwhile(4, halves)
         arrived(1, 7, other, 2, core, y_far)
         forward(1, 14)
+        meanwhile(4, halves)
         for h in (0, 1):
             for k, dy in ((8, 0), (12, 3), (13, 1), (14, 2)):
                 arrived(h, k, other, dy, 1 - core, partner)
@@ -254,25 +254,33 @@
         size = part_rows((0, 1, 1, 0, 0, 1)[k])[1]
         return pltpu.make_async_remote_copy(
             src_ref=codes.at[h, k, 0:size, :], dst_ref=landed.at[it, h, k, 0:size, :],
-            send_sem=x_send.at[it, h, k], recv_sem=x_recv.at[it, h, k],
+            send_sem=x_send.at[h, k], recv_sem=x_recv.at[it % 2, h, k],
             device_id=x_up if k % 2 == 0 else x_down, device_id_type=MESH,
         )
 
     def z_copy(it, h, d):
         return pltpu.make_async_remote_copy(
             src_ref=zcodes.at[h, (zl + d) % 4], dst_ref=zlanded.at[it, h, d - 1],
-            send_sem=z_send.at[it, h, d - 1], recv_sem=z_recv.at[it, h, d - 1],
+            send_sem=z_send.at[h, d - 1], recv_sem=z_recv.at[it % 2, h, d - 1],
             device_id=z_peers[d - 1], device_id_type=MESH,
         )
 
     def multiply_near(n, halves):
-        if n >= 3:
-            halves(2 * n - 6, 2 * n - 4)
+        if n == 3:
+            halves(1, 4)
+
+    def leave(h):
+        lanes = pl.ds(h * H, H)
+        return [
+            pltpu.make_async_copy(field.at[:, :, lanes], result.at[:, :, lanes], stage_sem.at[3 * h + n])
+            for n, (field, result) in enumerate(((wage, wage_out), (tech, tech_out), (temp, temp_out)))
+        ]
 
     def iteration(it, _):
-        def multiply(n):
-            product[n] = product[n] + jnp.dot(
-                folded[(x + n) % 4, other], supply_of(it, other), preferred_element_type=f32
+        def multiply(n, first=0, size=BLOCK):
+            rows = slice(first, first + size)
+            product[n, rows] = product[n, rows] + jnp.dot(
+                folded[(x + n) % 4, other, rows], supply_of(it, other), preferred_element_type=f32
             )
 
         def code(h, k, n, landing=None):
@@ -308,8 +316,9 @@
             for d in (2, 1, 3):
                 z_copy(it, h, d).start()
 
-        multiply(2)
+        multiply(2, *part_rows(0))
         code(0, 0, 2)
+        multiply(2, *part_rows(1))
         code(0, 1, 2)
         send_halo(it)
         multiply(1)
@@ -318,11 +327,13 @@
         code(0, 3, 3)
         code(1, 0, 2)
         code(1, 1, 2)
-        multiply(0)
         code(0, 4, 1, 0)
         code(0, 5, 3, 1)
         code(1, 2, 1)
         code(1, 3, 3)
+        for side in (zh, other):
+            value = jnp.dot(folded[x, side], supply_of(it, side), preferred_element_type=f32)
+            product[0] = value if side is zh else product[0] + value
         code(1, 4, 1, 0)
         code(1, 5, 3, 1)
         finish(0)
@@ -345,6 +356,13 @@
         for a in range(A):
             tech_new[0, a] = tech_new[0, a] - 0.05 * temp[a] * temp[a]
 
+        for copy in halo_copies(it):
+            copy.wait_send()
+        for h in (0, 1):
+            for copy in gather_copies(it, h):
+                copy().wait_send()
+            for k in range(6):
+                x_copy(it, h, k).wait_send()
         for h in (0, 1):
             for d in (1, 3, 2):
                 z_copy(it, h, d).wait_recv()
@@ -363,13 +381,12 @@
             def _():
                 send_supply(it + 1, h)
 
-        for copy in halo_copies(it):
-            copy.wait_send()
-        for h in (0, 1):
-            for copy in gather_copies(it, h):
-                copy().wait_send()
-            for k in range(6):
-                x_copy(it, h, k).wait_send()
+            @pl.when(it == ITERS - 1)
+            def _():
+                for copy in leave(h):
+                    copy.start()
+
+        for h in (0, 1):
             for d in (1, 2, 3):
                 z_copy(it, h, d).wait_send()
 
@@ -380,10 +397,13 @@
         return 0
 
     def build(n, halves):
-        if n < 4:
-            fold(n)
-        else:
-            halves(0, 4)
+        if n == 0:
+            fold(0)
+            fold(1)
+        elif n < 3:
+            fold(n + 1)
+        elif n == 4:
+            halves(1, 4)
 
     pl.semaphore_wait(barrier, len(peers))
     for copy in starts:
@@ -392,11 +412,22 @@
     send_supply(0, 1)
     gather(0, build)
     lax.fori_loop(0, ITERS, iteration, 0)
+    for h in (0, 1):
+        for copy in leave(h):
+            copy.wait()
 
 
 def hand_on(*refs):
-    for source, result in zip(refs[:3], refs[3:]):
-        result[...] = source[...]
+    sources, results, held, (sem,) = refs[0:3], refs[3:6], refs[6:9], refs[9:]
+    into = [pltpu.make_async_copy(sources[n], held[n], sem.at[0, n]) for n in range(3)]
+    out = [pltpu.make_async_copy(held[n], results[n], sem.at[1, n]) for n in range(3)]
+    for copy in into:
+        copy.start()
+    for n in range(3):
+        into[n].wait()
+        out[n].start()
+    for copy in out:
+        copy.wait()
 
 
 def local(cost_rough, land_mask, wage_start, tech_start, temp_start, damping):
@@ -408,8 +439,11 @@
         kernel,
         out_shape=(field, field, field),
         in_specs=[hbm, vmem, hbm, hbm, hbm, pl.BlockSpec(memory_space=pltpu.SMEM)],
-        out_specs=(vmem, vmem, vmem),
+        out_specs=(hbm, hbm, hbm),
         scratch_shapes=[
+            pltpu.VMEM((A, B, S), f32),
+            pltpu.VMEM((A, B, S), f32),
+            pltpu.VMEM((A, B, S), f32),
             pltpu.VMEM((A, LON, K), jnp.bfloat16),
             pltpu.VMEM((4, BLOCK, K), jnp.bfloat16),
             pltpu.VMEM((LON, K), f32),
@@ -430,14 +464,20 @@
             pltpu.VMEM((2, A, B, S), f32),
             dma((3,)),
             dma((A,)),
-            dma((ITERS, 2, 15)), dma((ITERS, 2, 15)),
-            dma((ITERS, 2, 6)), dma((ITERS, 2, 6)),
-            dma((ITERS, 2, 3)), dma((ITERS, 2, 3)),
-            dma((ITERS, 4)), dma((ITERS, 4)),
+            dma((2, 15)), dma((2, 2, 15)),
+            dma((2, 6)), dma((2, 2, 6)),
+            dma((2, 3)), dma((2, 2, 3)),
+            dma((4,)), dma((2, 4)),
         ],
         compiler_params=pltpu.CompilerParams(collective_id=0, has_side_effects=True, vmem_limit_bytes=60 * 1024 * 1024),
     )(cost_rough, land_mask, wage_start, tech_start, temp_start, damping)
-    return pl.pallas_call(hand_on, out_shape=(field, field, field), in_specs=[vmem] * 3, out_specs=(vmem,) * 3)(*fields)
+    return pl.pallas_call(
+        hand_on,
+        out_shape=(field, field, field),
+        in_specs=[hbm] * 3,
+        out_specs=(hbm,) * 3,
+        scratch_shapes=[pltpu.VMEM((A, B, S), f32)] * 3 + [dma((2, 3))],
+    )(*fields)
 
 
 def solution(mesh):

time: 113 us -> 109 us (0.965)
  Pallas kernels: 112 us -> 108 us
    pallas_call x1, Pallas kernels: 110 us -> 106 us  [local(): pl.pallas_call(kernel, out_shape=(field, field, field), in_specs=[hbm, vm...]
where the time goes in v3:
time: 109 us
  Pallas kernels  108 us (99%)
  between operations  1.29 us (1%)
    pallas_call x1, Pallas kernels, local(): pl.pallas_call(kernel, out_shape=(field, field, field), in_specs=[hbm, vm...  106 us

profile of v3, /device:TPU:1, one launch (start us, length us, event | category | flops | bytes accessed | tf_op | source)
XLA Modules:
  0.0 109.1 jit_solution(15586887740673465351)
XLA Ops:
  1.3 105.9 %shard_map.85 = (f32[11,12,256]{2,1,0:T(8,128)}, f32[11,12,256]{2,1,0:T(8,128)}, f32[11,12,256]{2,1,0:T(8,128)}) custom-call(bf16[2112,2112]{1,0:T(8,128)(2,1)} %rough.1, s32[11,12]{1,0:T(8,128)} %mask.1, f32[11,12,256]{2,1,0:T(8,128)} %wage0.1, f32[11,12,256]{2,1,0:T(8,128)} %tech0.1, f32[11,12,256]{2,1,0:T(8,128)} %temp0.1, f32[1]{0:T(128)S(6)} %copy.9.damping), custom_call_target="tpu_custom_call" | custom-call | tf_op jit(solution)/shard_map/pallas_call | solution.py:438
  107.2 1.8 %shard_map.86 = (f32[11,12,256]{2,1,0:T(8,128)}, f32[11,12,256]{2,1,0:T(8,128)}, f32[11,12,256]{2,1,0:T(8,128)}) custom-call(f32[11,12,256]{2,1,0:T(8,128)} %get-tuple-element.6.refs_0_, f32[11,12,256]{2,1,0:T(8,128)} %get-tuple-element.7.refs_1_, f32[11,12,256]{2,1,0:T(8,128)} %get-tuple-element.8.refs_2_), custom_call_target="tpu_custom_call" | custom-call | tf_op jit(solution)/shard_map/pallas_call | solution.py:474

commit v4 on v3

--- a/solution.py
+++ b/solution.py
@@ -21,7 +21,7 @@
 SIDE = 8 * PIECE
 WIDE = 3 * SIDE
 WINDOWS = ((0, 768, 0), (640, 768, 64), (1408, 704, 0))
-PARTS = ((0, 6), (6, 11))
+PARTS = (((0, 6), (6, 11)), ((0, 5), (5, 11)))
 FLAT = 144
 MESH = pl.DeviceIdType.MESH
 f32 = jnp.float32
@@ -167,15 +167,12 @@
         ]
         return [functools.partial(ag, it, h, *entry) for entry in table]
 
-    def halo_copies(it):
-        return [
-            pltpu.make_async_remote_copy(
-                src_ref=halo_out.at[it, d], dst_ref=halo_in.at[it, d],
-                send_sem=halo_send.at[d], recv_sem=halo_recv.at[it % 2, d],
-                device_id=peer, device_id_type=MESH,
-            )
-            for d, peer in enumerate(halo_peers)
-        ]
+    def halo_copy(it, d):
+        return pltpu.make_async_remote_copy(
+            src_ref=halo_out.at[it, d], dst_ref=halo_in.at[it, d],
+            send_sem=halo_send.at[d], recv_sem=halo_recv.at[it % 2, d],
+            device_id=halo_peers[d], device_id_type=MESH,
+        )
 
     def send_supply(it, h):
         for a in range(A):
@@ -188,15 +185,20 @@
         for copy in gather_copies(it, h)[0:5]:
             copy().start()
 
-    def send_halo(it):
+    def send_halo_rows(it):
         for f, field in enumerate((tech, temp)):
             halo_out[it, 0, f, 0:B, :] = field[A - 1]
             halo_out[it, 1, f, 0:B, :] = field[0]
+        for d in (0, 1):
+            halo_copy(it, d).start()
+
+    def send_halo_columns(it):
+        for f, field in enumerate((tech, temp)):
             for a in range(A):
                 halo_out[it, 2, f, a : a + 1, :] = field[a, B - 1 : B, :]
                 halo_out[it, 3, f, a : a + 1, :] = field[a, 0:1, :]
-        for copy in halo_copies(it):
-            copy.start()
+        for d in (2, 3):
+            halo_copy(it, d).start()
 
     def supply_of(it, side):
         return jnp.concatenate([gathered[it, side, h].reshape(WIDE, H) for h in (0, 1)], axis=1)
@@ -231,14 +233,15 @@
             forward(h, 5, 6, 7, 8)
             arrived(h, 3, zh, 2, core, y_far)
             forward(h, 11)
+        send_halo_columns(it)
         meanwhile(2, halves)
-        beside(0, other, 5, 12)
-        arrived(0, 7, other, 2, core, y_far)
-        forward(0, 14)
         for h in (0, 1):
             for k, dy in ((4, 0), (9, 3), (10, 1), (11, 2)):
                 arrived(h, k, zh, dy, 1 - core, partner)
         meanwhile(3, halves)
+        beside(0, other, 5, 12)
+        arrived(0, 7, other, 2, core, y_far)
+        forward(0, 14)
         beside(1, other, 5, 12)
         arrived(1, 7, other, 2, core, y_far)
         forward(1, 14)
@@ -247,11 +250,12 @@
             for k, dy in ((8, 0), (12, 3), (13, 1), (14, 2)):
                 arrived(h, k, other, dy, 1 - core, partner)
 
-    def part_rows(p):
-        return 48 * PARTS[p][0], 48 * (PARTS[p][1] - PARTS[p][0])
+    def part_rows(h, p):
+        first, last = PARTS[h][p]
+        return 48 * first, 48 * (last - first)
 
     def x_copy(it, h, k):
-        size = part_rows((0, 1, 1, 0, 0, 1)[k])[1]
+        size = part_rows(h, (0, 1, 1, 0, 0, 1)[k])[1]
         return pltpu.make_async_remote_copy(
             src_ref=codes.at[h, k, 0:size, :], dst_ref=landed.at[it, h, k, 0:size, :],
             send_sem=x_send.at[h, k], recv_sem=x_recv.at[it % 2, h, k],
@@ -267,7 +271,7 @@
 
     def multiply_near(n, halves):
         if n == 3:
-            halves(1, 4)
+            halves(1, 3)
 
     def leave(h):
         lanes = pl.ds(h * H, H)
@@ -285,7 +289,7 @@
 
         def code(h, k, n, landing=None):
             p = (0, 1, 1, 0, 0, 1)[k]
-            first, size = part_rows(p)
+            first, size = part_rows(h, p)
             if landing is not None:
                 x_copy(it, h, landing).wait_recv()
 
@@ -304,8 +308,8 @@
             for k in (2, 3, 4, 5):
                 x_copy(it, h, k).wait_recv()
             for p, pair in enumerate(((3, 4), (2, 5))):
-                for a in range(*PARTS[p]):
-                    rows = slice(48 * (a - PARTS[p][0]), 48 * (a - PARTS[p][0]) + 48)
+                for a in range(*PARTS[h][p]):
+                    rows = slice(48 * (a - PARTS[h][p][0]), 48 * (a - PARTS[h][p][0]) + 48)
                     value = product[0, 48 * a : 48 * a + 48, h * H : h * H + H]
                     for k in pair:
                         value = value + decode(landed[it, h, k, rows, :])
@@ -316,30 +320,33 @@
             for d in (2, 1, 3):
                 z_copy(it, h, d).start()
 
-        multiply(2, *part_rows(0))
+        def multiply_whole(n):
+            for side in (zh, other):
+                value = jnp.dot(folded[(x + n) % 4, side], supply_of(it, side), preferred_element_type=f32)
+                product[n] = value if side is zh else product[n] + value
+
+        multiply(2, *part_rows(0, 0))
         code(0, 0, 2)
-        multiply(2, *part_rows(1))
+        multiply(2, *part_rows(0, 1))
         code(0, 1, 2)
-        send_halo(it)
+        send_halo_rows(it)
         multiply(1)
         code(0, 2, 1)
-        multiply(3)
+        code(1, 1, 2)
+        multiply_whole(3)
         code(0, 3, 3)
         code(1, 0, 2)
-        code(1, 1, 2)
         code(0, 4, 1, 0)
         code(0, 5, 3, 1)
         code(1, 2, 1)
         code(1, 3, 3)
-        for side in (zh, other):
-            value = jnp.dot(folded[x, side], supply_of(it, side), preferred_element_type=f32)
-            product[0] = value if side is zh else product[0] + value
+        multiply_whole(0)
         code(1, 4, 1, 0)
         code(1, 5, 3, 1)
         finish(0)
         finish(1)
-        for copy in halo_copies(it):
-            copy.wait_recv()
+        for d in range(4):
+            halo_copy(it, d).wait_recv()
         for f, field in enumerate((tech, temp)):
             low = jnp.where(row == 0, 0.0, halo_in[it, 0, f, 0:B, :])
             high = jnp.where(row == 15, 0.0, halo_in[it, 1, f, 0:B, :])
@@ -356,8 +363,8 @@
         for a in range(A):
             tech_new[0, a] = tech_new[0, a] - 0.05 * temp[a] * temp[a]
 
-        for copy in halo_copies(it):
-            copy.wait_send()
+        for d in range(4):
+            halo_copy(it, d).wait_send()
         for h in (0, 1):
             for copy in gather_copies(it, h):
                 copy().wait_send()
@@ -400,10 +407,11 @@
         if n == 0:
             fold(0)
             fold(1)
-        elif n < 3:
-            fold(n + 1)
+        elif n == 2:
+            fold(2)
+            fold(3)
         elif n == 4:
-            halves(1, 4)
+            halves(1, 3)
 
     pl.semaphore_wait(barrier, len(peers))
     for copy in starts:

time: 109 us -> 108 us (level)
  Pallas kernels: 108 us -> 106 us
    pallas_call x1, Pallas kernels: 106 us -> 105 us  [local(): pl.pallas_call(kernel, out_shape=(field, field, field), in_specs=[hbm, vm...]
where the time goes in v4:
time: 108 us
  Pallas kernels  106 us (98%)
  between operations  1.29 us (1%)
    pallas_call x1, Pallas kernels, local(): pl.pallas_call(kernel, out_shape=(field, field, field), in_specs=[hbm, vm...  105 us

profile of v4, /device:TPU:1, one launch (start us, length us, event | category | flops | bytes accessed | tf_op | source)
XLA Modules:
  0.0 107.8 jit_solution(481413900902453670)
XLA Ops:
  1.3 104.7 %shard_map.85 = (f32[11,12,256]{2,1,0:T(8,128)}, f32[11,12,256]{2,1,0:T(8,128)}, f32[11,12,256]{2,1,0:T(8,128)}) custom-call(bf16[2112,2112]{1,0:T(8,128)(2,1)} %rough.1, s32[11,12]{1,0:T(8,128)} %mask.1, f32[11,12,256]{2,1,0:T(8,128)} %wage0.1, f32[11,12,256]{2,1,0:T(8,128)} %tech0.1, f32[11,12,256]{2,1,0:T(8,128)} %temp0.1, f32[1]{0:T(128)S(6)} %copy.9.damping), custom_call_target="tpu_custom_call" | custom-call | tf_op jit(solution)/shard_map/pallas_call | solution.py:446
  105.9 1.8 %shard_map.86 = (f32[11,12,256]{2,1,0:T(8,128)}, f32[11,12,256]{2,1,0:T(8,128)}, f32[11,12,256]{2,1,0:T(8,128)}) custom-call(f32[11,12,256]{2,1,0:T(8,128)} %get-tuple-element.6.refs_0_, f32[11,12,256]{2,1,0:T(8,128)} %get-tuple-element.7.refs_1_, f32[11,12,256]{2,1,0:T(8,128)} %get-tuple-element.8.refs_2_), custom_call_target="tpu_custom_call" | custom-call | tf_op jit(solution)/shard_map/pallas_call | solution.py:482

commit v5 on v4

--- a/solution.py
+++ b/solution.py
@@ -23,6 +23,7 @@
 WINDOWS = ((0, 768, 0), (640, 768, 64), (1408, 704, 0))
 PARTS = (((0, 6), (6, 11)), ((0, 5), (5, 11)))
 FLAT = 144
+FLAT_ROWS = (slice(0, 80), slice(80, 144))
 MESH = pl.DeviceIdType.MESH
 f32 = jnp.float32
 STEPS = 1024.0
@@ -254,18 +255,37 @@
         first, last = PARTS[h][p]
         return 48 * first, 48 * (last - first)
 
-    def x_copy(it, h, k):
-        size = part_rows(h, (0, 1, 1, 0, 0, 1)[k])[1]
+    def piece_of(h, p, s):
+        first, last = PARTS[h][p]
+        middle = first + (last - first + 1) // 2
+        return ((first, middle), (middle, last))[s]
+
+    def places(h, s):
+        latitudes = [a for p in (0, 1) for a in range(*piece_of(h, p, s))]
+        return {a: FLAT_ROWS[s].start + B * n for n, a in enumerate(latitudes)}
+
+    def x_rows(h, k, s):
+        p = (0, 1, 1, 0, 0, 1)[k]
+        first, last = PARTS[h][p] if s is None else piece_of(h, p, s)
+        return 48 * (first - PARTS[h][p][0]), 48 * (last - first)
+
+    def x_copy(it, h, k, s=None):
+        first, size = x_rows(h, k, s)
+        sem = k if s is None else 2 * k - 4 + s
         return pltpu.make_async_remote_copy(
-            src_ref=codes.at[h, k, 0:size, :], dst_ref=landed.at[it, h, k, 0:size, :],
-            send_sem=x_send.at[h, k], recv_sem=x_recv.at[it % 2, h, k],
+            src_ref=codes.at[h, k, pl.ds(first, size), :], dst_ref=landed.at[it, h, k, pl.ds(first, size), :],
+            send_sem=x_send.at[h, sem], recv_sem=x_recv.at[it % 2, h, sem],
             device_id=x_up if k % 2 == 0 else x_down, device_id_type=MESH,
         )
 
-    def z_copy(it, h, d):
+    def x_copies(it, h):
+        return [x_copy(it, h, k) for k in range(4)] + [x_copy(it, h, k, s) for k in (4, 5) for s in (0, 1)]
+
+    def z_copy(it, h, s, d):
+        rows = pl.ds(FLAT_ROWS[s].start, FLAT_ROWS[s].stop - FLAT_ROWS[s].start)
         return pltpu.make_async_remote_copy(
-            src_ref=zcodes.at[h, (zl + d) % 4], dst_ref=zlanded.at[it, h, d - 1],
-            send_sem=z_send.at[h, d - 1], recv_sem=z_recv.at[it % 2, h, d - 1],
+            src_ref=zcodes.at[h, (zl + d) % 4, rows, :], dst_ref=zlanded.at[it, h, d - 1, rows, :],
+            send_sem=z_send.at[h, s, d - 1], recv_sem=z_recv.at[it % 2, h, s, d - 1],
             device_id=z_peers[d - 1], device_id_type=MESH,
         )
 
@@ -287,38 +307,48 @@
                 folded[(x + n) % 4, other, rows], supply_of(it, other), preferred_element_type=f32
             )
 
-        def code(h, k, n, landing=None):
-            p = (0, 1, 1, 0, 0, 1)[k]
-            first, size = part_rows(h, p)
-            if landing is not None:
-                x_copy(it, h, landing).wait_recv()
+        def code(h, k, n, landing=None, s=None):
+            base = 48 * PARTS[h][(0, 1, 1, 0, 0, 1)[k]][0]
+            first, size = x_rows(h, k, s)
 
             def some(i, _):
-                start = pl.multiple_of(i * 48, 16)
-                value = product[n, pl.ds(first + start, 48), h * H : h * H + H]
+                start = pl.multiple_of(first + i * 48, 16)
+                value = product[n, pl.ds(base + start, 48), h * H : h * H + H]
                 if landing is not None:
                     value = value + decode(landed[it, h, landing, pl.ds(start, 48), :])
                 codes[h, k, pl.ds(start, 48), :] = encode(value)
                 return 0
 
             lax.fori_loop(0, size // 48, some, 0)
-            x_copy(it, h, k).start()
-
-        def finish(h):
-            for k in (2, 3, 4, 5):
-                x_copy(it, h, k).wait_recv()
+            x_copy(it, h, k, s).start()
+
+        def relay(h):
+            x_copy(it, h, 0).wait_recv()
+            code(h, 4, 1, 0, 0)
+            x_copy(it, h, 1).wait_recv()
+            code(h, 5, 3, 1, 0)
+            code(h, 4, 1, 0, 1)
+            code(h, 5, 3, 1, 1)
+
+        def finish(h, s):
+            if s == 0:
+                for k in (2, 3):
+                    x_copy(it, h, k).wait_recv()
+            for k in (4, 5):
+                x_copy(it, h, k, s).wait_recv()
             for p, pair in enumerate(((3, 4), (2, 5))):
-                for a in range(*PARTS[h][p]):
+                for a in range(*piece_of(h, p, s)):
                     rows = slice(48 * (a - PARTS[h][p][0]), 48 * (a - PARTS[h][p][0]) + 48)
                     value = product[0, 48 * a : 48 * a + 48, h * H : h * H + H]
                     for k in pair:
                         value = value + decode(landed[it, h, k, rows, :])
+                    put = places(h, s)[a]
                     for z in range(4):
-                        flat[h, z, B * a : B * a + B, :] = value[B * z : B * z + B, :]
+                        flat[h, z, put : put + B, :] = value[B * z : B * z + B, :]
             for z in range(4):
-                zcodes[h, z] = encode(flat[h, z])
+                zcodes[h, z, FLAT_ROWS[s], :] = encode(flat[h, z, FLAT_ROWS[s], :])
             for d in (2, 1, 3):
-                z_copy(it, h, d).start()
+                z_copy(it, h, s, d).start()
 
         def multiply_whole(n):
             for side in (zh, other):
@@ -336,15 +366,15 @@
         multiply_whole(3)
         code(0, 3, 3)
         code(1, 0, 2)
-        code(0, 4, 1, 0)
-        code(0, 5, 3, 1)
+        relay(0)
         code(1, 2, 1)
         code(1, 3, 3)
         multiply_whole(0)
-        code(1, 4, 1, 0)
-        code(1, 5, 3, 1)
-        finish(0)
-        finish(1)
+        relay(1)
+        finish(0, 0)
+        finish(0, 1)
+        finish(1, 0)
+        finish(1, 1)
         for d in range(4):
             halo_copy(it, d).wait_recv()
         for f, field in enumerate((tech, temp)):
@@ -368,17 +398,19 @@
         for h in (0, 1):
             for copy in gather_copies(it, h):
                 copy().wait_send()
-            for k in range(6):
-                x_copy(it, h, k).wait_send()
+            for copy in x_copies(it, h):
+                copy.wait_send()
         for h in (0, 1):
-            for d in (1, 3, 2):
-                z_copy(it, h, d).wait_recv()
+            for s in (0, 1):
+                for d in (1, 3, 2):
+                    z_copy(it, h, s, d).wait_recv()
             lanes = slice(h * H, h * H + H)
             total = flat[h, zl]
             for d in (1, 2, 3):
                 total = total + decode(zlanded[it, h, d - 1])
+            where = {**places(h, 0), **places(h, 1)}
             for a in range(A):
-                target_ = 0.5 * (jnp.log(total[B * a : B * a + B, :]) + tech[a, :, lanes])
+                target_ = 0.5 * (jnp.log(total[where[a] : where[a] + B, :]) + tech[a, :, lanes])
                 wage_a = wage[a, :, lanes] + damping[0] * (target_ - wage[a, :, lanes])
                 wage[a, :, lanes] = wage_a
                 temp[a, :, lanes] = tech_new[1, a, :, lanes] + 0.5 * share[a, :, lanes] * jnp.tanh(wage_a)
@@ -394,8 +426,9 @@
                     copy.start()
 
         for h in (0, 1):
-            for d in (1, 2, 3):
-                z_copy(it, h, d).wait_send()
+            for s in (0, 1):
+                for d in (1, 2, 3):
+                    z_copy(it, h, s, d).wait_send()
 
         @pl.when(it < ITERS - 1)
         def _():
@@ -473,8 +506,8 @@
             dma((3,)),
             dma((A,)),
             dma((2, 15)), dma((2, 2, 15)),
-            dma((2, 6)), dma((2, 2, 6)),
-            dma((2, 3)), dma((2, 2, 3)),
+            dma((2, 8)), dma((2, 2, 8)),
+            dma((2, 2, 3)), dma((2, 2, 2, 3)),
             dma((4,)), dma((2, 4)),
         ],
         compiler_params=pltpu.CompilerParams(collective_id=0, has_side_effects=True, vmem_limit_bytes=60 * 1024 * 1024),

time: 108 us -> 107 us (level)
  no operation moved by 1% of the time
where the time goes in v5:
time: 107 us
  Pallas kernels  105 us (98%)
  between operations  1.29 us (1%)
    pallas_call x1, Pallas kernels, local(): pl.pallas_call(kernel, out_shape=(field, field, field), in_specs=[hbm, vm...  104 us

profile of v5, /device:TPU:1, one launch (start us, length us, event | category | flops | bytes accessed | tf_op | source)
XLA Modules:
  0.0 106.7 jit_solution(1151026480009200120)
XLA Ops:
  1.3 103.6 %shard_map.85 = (f32[11,12,256]{2,1,0:T(8,128)}, f32[11,12,256]{2,1,0:T(8,128)}, f32[11,12,256]{2,1,0:T(8,128)}) custom-call(bf16[2112,2112]{1,0:T(8,128)(2,1)} %rough.1, s32[11,12]{1,0:T(8,128)} %mask.1, f32[11,12,256]{2,1,0:T(8,128)} %wage0.1, f32[11,12,256]{2,1,0:T(8,128)} %tech0.1, f32[11,12,256]{2,1,0:T(8,128)} %temp0.1, f32[1]{0:T(128)S(6)} %copy.9.damping), custom_call_target="tpu_custom_call" | custom-call | tf_op jit(solution)/shard_map/pallas_call | solution.py:479
  104.9 1.8 %shard_map.86 = (f32[11,12,256]{2,1,0:T(8,128)}, f32[11,12,256]{2,1,0:T(8,128)}, f32[11,12,256]{2,1,0:T(8,128)}) custom-call(f32[11,12,256]{2,1,0:T(8,128)} %get-tuple-element.6.refs_0_, f32[11,12,256]{2,1,0:T(8,128)} %get-tuple-element.7.refs_1_, f32[11,12,256]{2,1,0:T(8,128)} %get-tuple-element.8.refs_2_), custom_call_target="tpu_custom_call" | custom-call | tf_op jit(solution)/shard_map/pallas_call | solution.py:515

commit v6 on v5

--- a/solution.py
+++ b/solution.py
@@ -89,23 +89,6 @@
         stand = jnp.sum(jnp.where(diagonal, line, 0.0), axis=1, keepdims=True)
         share[a] = jnp.broadcast_to(0.25 + stand, (B, S))
 
-    spot = lax.broadcasted_iota(jnp.int32, (1, 16 * PIECE), 1)
-    device = jnp.zeros_like(spot)
-    for r in range(1, 16):
-        device = device + (spot >= PIECE * r).astype(jnp.int32)
-    rest = spot - PIECE * device
-    target = (rest & 3) * LAT + A * device + (rest >> 2)
-    target = jnp.where(rest < 4 * A, target, -4096)
-
-    def pick_rows(i, _):
-        start = pl.multiple_of(i * 16, 16)
-        rows = i * 16 + lax.broadcasted_iota(jnp.int32, (16, 16 * PIECE), 0)
-        for n, shift in enumerate((0, 64)):
-            pick[n, pl.ds(start, 16), :] = jnp.where(rows == target + shift, 1.0, 0.0).astype(jnp.bfloat16)
-        return 0
-
-    lax.fori_loop(0, PIECE, pick_rows, 0)
-
     column = lax.broadcasted_iota(jnp.int32, (1, K), 1)
     local_b = jnp.zeros_like(column)
     for b in range(1, B):
@@ -134,7 +117,7 @@
 
         return lax.fori_loop(0, LON // 16, cost_rows, 0)
 
-    lax.fori_loop(0, A, cost_latitude, 0)
+    lax.fori_loop(0, 7, cost_latitude, 0)
 
     def fold(n):
         for g, (first, count, shift) in enumerate(WINDOWS):
@@ -451,6 +434,25 @@
         copy.wait()
     send_supply(0, 0)
     send_supply(0, 1)
+
+    spot = lax.broadcasted_iota(jnp.int32, (1, 16 * PIECE), 1)
+    device = jnp.zeros_like(spot)
+    for r in range(1, 16):
+        device = device + (spot >= PIECE * r).astype(jnp.int32)
+    rest = spot - PIECE * device
+    target = (rest & 3) * LAT + A * device + (rest >> 2)
+    target = jnp.where(rest < 4 * A, target, -4096)
+
+    def pick_rows(i, _):
+        start = pl.multiple_of(i * 16, 16)
+        rows = i * 16 + lax.broadcasted_iota(jnp.int32, (16, 16 * PIECE), 0)
+        for n, shift in enumerate((0, 64)):
+            pick[n, pl.ds(start, 16), :] = jnp.where(rows == target + shift, 1.0, 0.0).astype(jnp.bfloat16)
+        return 0
+
+    lax.fori_loop(0, PIECE, pick_rows, 0)
+
+    lax.fori_loop(7, A, cost_latitude, 0)
     gather(0, build)
     lax.fori_loop(0, ITERS, iteration, 0)
     for h in (0, 1):

time: 107 us -> 102 us (0.953)
  Pallas kernels: 105 us -> 101 us
    pallas_call x1, Pallas kernels: 104 us -> 99.2 us  [local(): pl.pallas_call(kernel, out_shape=(field, field, field), in_specs=[hbm, vm...]
where the time goes in v6:
time: 102 us
  Pallas kernels  101 us (99%)
  between operations  1.29 us (1%)
    pallas_call x1, Pallas kernels, local(): pl.pallas_call(kernel, out_shape=(field, field, field), in_specs=[hbm, vm...  99.2 us

profile of v6, /device:TPU:1, one launch (start us, length us, event | category | flops | bytes accessed | tf_op | source)
XLA Modules:
  0.0 102.3 jit_solution(15587983643099895007)
XLA Ops:
  1.3 99.2 %shard_map.85 = (f32[11,12,256]{2,1,0:T(8,128)}, f32[11,12,256]{2,1,0:T(8,128)}, f32[11,12,256]{2,1,0:T(8,128)}) custom-call(bf16[2112,2112]{1,0:T(8,128)(2,1)} %rough.1, s32[11,12]{1,0:T(8,128)} %mask.1, f32[11,12,256]{2,1,0:T(8,128)} %wage0.1, f32[11,12,256]{2,1,0:T(8,128)} %tech0.1, f32[11,12,256]{2,1,0:T(8,128)} %temp0.1, f32[1]{0:T(128)S(6)} %copy.9.damping), custom_call_target="tpu_custom_call" | custom-call | tf_op jit(solution)/shard_map/pallas_call | solution.py:481
  100.5 1.8 %shard_map.86 = (f32[11,12,256]{2,1,0:T(8,128)}, f32[11,12,256]{2,1,0:T(8,128)}, f32[11,12,256]{2,1,0:T(8,128)}) custom-call(f32[11,12,256]{2,1,0:T(8,128)} %get-tuple-element.6.refs_0_, f32[11,12,256]{2,1,0:T(8,128)} %get-tuple-element.7.refs_1_, f32[11,12,256]{2,1,0:T(8,128)} %get-tuple-element.8.refs_2_), custom_call_target="tpu_custom_call" | custom-call | tf_op jit(solution)/shard_map/pallas_call | solution.py:517
